TPU v7x, 256 devices: a whole 4x4x8 slice. The times are simulated.
256 devices in a mesh: seq: 64 (over z, y, core), dp: 4 (over x).
Axes of the slice: x: 4, y: 4, z: 8, core: 2. Of those that a mesh axis runs over, the one named last changes fastest.
Arguments:
- signal: bfloat16 [4, 65536, 384], P('dp', 'seq'), may hold values from -6 to 6
- filter_raw: bfloat16 [65536, 384], P('seq'), may hold values from -6 to 6
- cotangent: bfloat16 [4, 65536, 384], P('dp', 'seq'), may hold values from -6 to 6
- block_mask: int32 [4, 64], P('dp', 'seq'), may hold values from 0 to 1, as said below
Outputs:
- conv_out: bfloat16 [4, 65536, 384], P('dp', 'seq')
- signal_grad: bfloat16 [4, 65536, 384], P('dp', 'seq')
- filter_grad: bfloat16 [65536, 384], P('seq')
Inputs may be any that keep to these rules, and one draw needn't show every extreme that they name: `block_mask`: each sequence's row is 1 on a leading run of blocks and 0 on the rest; every row has both.
All inputs are finite; a program needn't handle non-finite values.
Results may differ from a plain program's by a relative error of at most 0.013.
Values may be sent and summed in bfloat16 or wider, within the bound.
A program may use at most 128 MiB of HBM per device.

v0:
```python
import math

import jax
import jax.numpy as jnp
from jax import lax
from jax.sharding import PartitionSpec as P

BLK = 1024
RAD = 32


def angle_table(row_ids, col_ids, period):
    product = row_ids[:, None] * col_ids[None, :] % period
    return 2.0 * math.pi / period * product.astype(jnp.float32)


def per_device(signal, filter_raw, cotangent, block_mask):
    tokens = filter_raw.shape[0]
    channels = filter_raw.shape[1]
    seq_count = lax.axis_size("seq")
    seq_index = lax.axis_index("seq")
    local_blocks = tokens // BLK
    real_blocks = local_blocks * seq_count
    all_blocks = 2 * real_blocks
    column_width = BLK // seq_count
    freq_width = all_blocks // seq_count
    period = all_blocks * BLK
    freq_ids = jnp.arange(all_blocks, dtype=jnp.int32)
    block_ids = jnp.arange(real_blocks, dtype=jnp.int32)
    radix_ids = jnp.arange(RAD, dtype=jnp.int32)
    outer_angle = angle_table(freq_ids, block_ids, all_blocks)
    cos_one = jnp.cos(outer_angle).astype(jnp.bfloat16)
    sin_one = jnp.sin(outer_angle).astype(jnp.bfloat16)
    radix_angle = angle_table(radix_ids, radix_ids, RAD)
    cos_rad = jnp.cos(radix_angle).astype(jnp.bfloat16)
    sin_rad = jnp.sin(radix_angle).astype(jnp.bfloat16)
    inner_angle = angle_table(radix_ids, radix_ids, BLK)
    inner_cos = jnp.cos(inner_angle)[None, :, :, None]
    inner_sin = jnp.sin(inner_angle)[None, :, :, None]
    column_ids = seq_index * column_width + jnp.arange(column_width, dtype=jnp.int32)
    column_angle = angle_table(freq_ids, column_ids, period)
    column_cos = jnp.cos(column_angle)[:, :, None]
    column_sin = jnp.sin(column_angle)[:, :, None]
    own_freqs = seq_index * freq_width + jnp.arange(freq_width, dtype=jnp.int32)
    freq_angle = angle_table(own_freqs, jnp.arange(BLK, dtype=jnp.int32), period)
    freq_cos = jnp.cos(freq_angle)[:, :, None]
    freq_sin = jnp.sin(freq_angle)[:, :, None]
    factor = 1.0 / (all_blocks * BLK * math.sqrt(real_blocks * BLK))

    def outer_section(portion):
        first_real = jnp.einsum("ka,abc->kbc", cos_one, portion, preferred_element_type=jnp.float32)
        first_imag = -jnp.einsum(
            "ka,abc->kbc", sin_one, portion, preferred_element_type=jnp.float32
        )
        turned_real = first_real * column_cos + first_imag * column_sin
        turned_imag = first_imag * column_cos - first_real * column_sin
        return jnp.stack([turned_real, turned_imag]).astype(jnp.bfloat16)

    def inner_section(portion):
        rows_here = portion.shape[1]
        width = portion.shape[3]
        parted = portion.reshape(2, rows_here, RAD, RAD, width)
        mid_real = jnp.einsum(
            "pr,kpqc->krqc", cos_rad, parted[0], preferred_element_type=jnp.float32
        ) + jnp.einsum("pr,kpqc->krqc", sin_rad, parted[1], preferred_element_type=jnp.float32)
        mid_imag = jnp.einsum(
            "pr,kpqc->krqc", cos_rad, parted[1], preferred_element_type=jnp.float32
        ) - jnp.einsum("pr,kpqc->krqc", sin_rad, parted[0], preferred_element_type=jnp.float32)
        spun_real = (mid_real * inner_cos + mid_imag * inner_sin).astype(jnp.bfloat16)
        spun_imag = (mid_imag * inner_cos - mid_real * inner_sin).astype(jnp.bfloat16)
        last_real = jnp.einsum(
            "qs,krqc->ksrc", cos_rad, spun_real, preferred_element_type=jnp.float32
        ) + jnp.einsum("qs,krqc->ksrc", sin_rad, spun_imag, preferred_element_type=jnp.float32)
        last_imag = jnp.einsum(
            "qs,krqc->ksrc", cos_rad, spun_imag, preferred_element_type=jnp.float32
        ) - jnp.einsum("qs,krqc->ksrc", sin_rad, spun_real, preferred_element_type=jnp.float32)
        return jnp.stack([last_real, last_imag]).reshape(2, rows_here, BLK, width)

    def forward(values):
        spread = outer_section(
            lax.all_to_all(values, "seq", split_axis=1, concat_axis=0, tiled=True)
        )
        return inner_section(lax.all_to_all(spread, "seq", split_axis=1, concat_axis=2, tiled=True))

    def outer_back(portion):
        combined = jnp.einsum(
            "ka,kbc->abc", cos_one, portion[0], preferred_element_type=jnp.float32
        ) - jnp.einsum("ka,kbc->abc", sin_one, portion[1], preferred_element_type=jnp.float32)
        return (combined * factor).astype(jnp.bfloat16)

    def inverse(spectrum):
        width = spectrum.shape[3]
        rounded_spec = spectrum.astype(jnp.bfloat16).reshape(2, freq_width, RAD, RAD, width)
        mid_real = jnp.einsum(
            "sq,ksrc->krqc", cos_rad, rounded_spec[0], preferred_element_type=jnp.float32
        ) - jnp.einsum(
            "sq,ksrc->krqc", sin_rad, rounded_spec[1], preferred_element_type=jnp.float32
        )
        mid_imag = jnp.einsum(
            "sq,ksrc->krqc", cos_rad, rounded_spec[1], preferred_element_type=jnp.float32
        ) + jnp.einsum(
            "sq,ksrc->krqc", sin_rad, rounded_spec[0], preferred_element_type=jnp.float32
        )
        spun_real = (mid_real * inner_cos - mid_imag * inner_sin).astype(jnp.bfloat16)
        spun_imag = (mid_imag * inner_cos + mid_real * inner_sin).astype(jnp.bfloat16)
        back_real = jnp.einsum(
            "rp,krqc->kpqc", cos_rad, spun_real, preferred_element_type=jnp.float32
        ) - jnp.einsum("rp,krqc->kpqc", sin_rad, spun_imag, preferred_element_type=jnp.float32)
        back_imag = jnp.einsum(
            "rp,krqc->kpqc", cos_rad, spun_imag, preferred_element_type=jnp.float32
        ) + jnp.einsum("rp,krqc->kpqc", sin_rad, spun_real, preferred_element_type=jnp.float32)
        back_real = back_real.reshape(freq_width, BLK, width)
        back_imag = back_imag.reshape(freq_width, BLK, width)
        turned_real = back_real * freq_cos - back_imag * freq_sin
        turned_imag = back_imag * freq_cos + back_real * freq_sin
        packed = jnp.stack([turned_real, turned_imag]).astype(jnp.bfloat16)
        columns = outer_back(lax.all_to_all(packed, "seq", split_axis=2, concat_axis=1, tiled=True))
        return lax.all_to_all(columns, "seq", split_axis=0, concat_axis=1, tiled=True)

    mask_blocks = block_mask[0].astype(jnp.bfloat16)[:, None, None]
    masked = signal[0].reshape(local_blocks, BLK, channels) * mask_blocks
    grad_input = cotangent[0].reshape(local_blocks, BLK, channels)
    filter_input = filter_raw.reshape(local_blocks, BLK, channels)
    spec_signal = forward(masked)
    spec_grad = forward(grad_input)
    spec_filter = forward(filter_input)
    signal_real, signal_imag = (spec_signal[0], spec_signal[1])
    filter_real, filter_imag = (spec_filter[0], spec_filter[1])
    grad_real, grad_imag = (spec_grad[0], spec_grad[1])
    spec_out = jnp.stack(
        [
            signal_real * filter_real - signal_imag * filter_imag,
            signal_real * filter_imag + signal_imag * filter_real,
        ]
    )
    spec_input = jnp.stack(
        [
            grad_real * filter_real + grad_imag * filter_imag,
            grad_imag * filter_real - grad_real * filter_imag,
        ]
    )
    spec_weight = jnp.stack(
        [
            grad_real * signal_real + grad_imag * signal_imag,
            grad_imag * signal_real - grad_real * signal_imag,
        ]
    )
    weight_total = lax.psum(spec_weight.astype(jnp.bfloat16), "dp").astype(jnp.float32)
    conv_rows = inverse(spec_out)
    input_rows = inverse(spec_input)
    weight_rows = inverse(weight_total)
    input_rows = input_rows * mask_blocks
    return (conv_rows, input_rows, weight_rows.reshape(tokens, channels))


def solution(mesh):
    placed = (P("dp", "seq", None), P("seq", None), P("dp", "seq", None), P("dp", "seq"))
    return jax.shard_map(
        per_device,
        mesh=mesh,
        in_specs=placed,
        out_specs=(P("dp", "seq", None), P("dp", "seq", None), P("seq", None)),
        check_vma=False,
    )
```

profile of v0, /device:TPU:1, one launch (start us, length us, event | category | flops | bytes accessed | tf_op | source)
XLA Modules:
  0.0 879.8 jit_solution(18364543493127519809)
XLA Ops:
  10.0 5.4 reduce
  16.5 13.7 %all-to-all-start.6 = ((bf16[64,2,3072]{2,1,0:T(2,128)(2,1)}), bf16[64,2,3072]{2,1,0:T(2,128)(2,1)S(1)}, u32[]{:S(2)}, u32[]{:S(2)}) async-start(bf16[64,2,3072]{2,1,0:T(2,128)(2,1)} %reshape.688), calls=%async_computation.6 | async-start | bytes 1572864 | tf_op jit(solution)/shard_map/all_to_all | solution.py:81
  31.5 5.4 reduce.1
  38.0 15.1 %all-to-all-done.6 = bf16[64,2,3072]{2,1,0:T(2,128)(2,1)S(1)} async-done(((bf16[64,2,3072]{2,1,0:T(2,128)(2,1)}), bf16[64,2,3072]{2,1,0:T(2,128)(2,1)S(1)}, u32[]{:S(2)}, u32[]{:S(2)}) %all-to-all-start.6) | async-done | bytes 786464 | tf_op jit(solution)/shard_map/all_to_all | solution.py:81
  53.1 6.8 all-to-all-start.2
  62.2 5.4 reduce.2
  68.7 13.9 %all-to-all-done.2 = bf16[64,2,3072]{2,1,0:T(2,128)(2,1)} async-done(((bf16[64,2,3072]{2,1,0:T(2,128)(2,1)}), bf16[64,2,3072]{2,1,0:T(2,128)(2,1)}, u32[]{:S(2)}, u32[]{:S(2)}) %all-to-all-start.2) | async-done | bytes 786464 | tf_op jit(solution)/shard_map/all_to_all | solution.py:81
  82.6 6.4 all-to-all-start
  90.9 4.9 reshape.687
  104.9 6.9 all-to-all-done
  111.8 5.8 reshape.685
  121.4 6.4 fusion.20
  128.1 3.5 copy.180
  131.6 6.2 all-to-all-start.1
  140.1 3.5 copy.193
  143.6 66.5 %all-to-all-done.1 = bf16[2,128,16,384]{3,2,0,1:T(8,128)(2,1)S(1)} async-done(((bf16[2,128,16,384]{3,2,0,1:T(8,128)(2,1)}), bf16[2,128,16,384]{3,2,0,1:T(8,128)(2,1)S(1)}, u32[]{:S(2)}, u32[]{:S(2)}) %all-to-all-start.1) | async-done | bytes 3145760 | tf_op jit(solution)/shard_map/all_to_all | solution.py:83
  211.8 6.9 all-to-all-start.3
  221.0 3.5 copy.223
  224.5 66.8 %all-to-all-done.3 = bf16[2,128,16,384]{3,2,0,1:T(8,128)(2,1)} async-done(((bf16[2,128,16,384]{3,2,0,1:T(8,128)(2,1)}), bf16[2,128,16,384]{3,2,0,1:T(8,128)(2,1)}, u32[]{:S(2)}, u32[]{:S(2)}) %all-to-all-start.3) | async-done | bytes 3145760 | tf_op jit(solution)/shard_map/all_to_all | solution.py:83
  291.3 6.6 all-to-all-start.7
  316.9 53.4 %all-to-all-done.7 = bf16[2,128,16,384]{3,2,0,1:T(8,128)(2,1)S(1)} async-done(((bf16[2,128,16,384]{3,2,0,1:T(8,128)(2,1)}), bf16[2,128,16,384]{3,2,0,1:T(8,128)(2,1)S(1)}, u32[]{:S(2)}, u32[]{:S(2)}) %all-to-all-start.7) | async-done | bytes 3145760 | tf_op jit(solution)/shard_map/all_to_all | solution.py:83
  376.7 6.5 fusion.3
  394.7 6.7 fusion.26
  417.7 65.2 %all-reduce.2.cloned.1.call-done = bf16[2,2,1024,384]{3,2,1,0:T(8,128)(2,1)} async-done(((bf16[2,2,1024,384]{3,2,1,0:T(8,128)(2,1)}), bf16[2,2,1024,384]{3,2,1,0:T(8,128)(2,1)}) %all-reduce.2.cloned.1.call-update) | async-done | bytes 3145744 | tf_op jit(solution)/shard_map/psum | solution.py:148
  493.0 6.8 fusion.29
  520.2 4.5 subtract_convert_fusion
  525.1 4.9 copy.258
  530.0 10.9 %all-to-all-start.10 = ((bf16[2,2,1024,384]{3,1,0,2:T(2,128)(2,1)}), bf16[2,2,1024,384]{3,1,0,2:T(2,128)(2,1)S(1)}, u32[]{:S(2)}, u32[]{:S(2)}) async-start(bf16[2,2,1024,384]{3,1,0,2:T(2,128)(2,1)} %copy.258), calls=%async_computation.10 | async-start | bytes 6291456 | tf_op jit(solution)/shard_map/all_to_all | solution.py:117
  543.1 4.9 copy.241
  548.0 65.3 %all-to-all-done.10 = bf16[2,2,1024,384]{3,1,0,2:T(2,128)(2,1)S(1)} async-done(((bf16[2,2,1024,384]{3,1,0,2:T(2,128)(2,1)}), bf16[2,2,1024,384]{3,1,0,2:T(2,128)(2,1)S(1)}, u32[]{:S(2)}, u32[]{:S(2)}) %all-to-all-start.10) | async-done | bytes 3145760 | tf_op jit(solution)/shard_map/all_to_all | solution.py:117
  615.0 6.7 all-to-all-start.8
  624.0 4.9 copy.215
  628.9 65.3 %all-to-all-done.8 = bf16[2,2,1024,384]{3,1,0,2:T(2,128)(2,1)S(1)} async-done(((bf16[2,2,1024,384]{3,1,0,2:T(2,128)(2,1)}), bf16[2,2,1024,384]{3,1,0,2:T(2,128)(2,1)S(1)}, u32[]{:S(2)}, u32[]{:S(2)}) %all-to-all-start.8) | async-done | bytes 3145760 | tf_op jit(solution)/shard_map/all_to_all | solution.py:117
  694.2 7.5 all-to-all-start.4
  708.2 4.7 squeeze.77
  712.9 4.2 copy.261
  717.1 4.6 squeeze.78
  725.6 48.5 %all-to-all-done.4 = bf16[2,2,1024,384]{3,1,0,2:T(2,128)(2,1)} async-done(((bf16[2,2,1024,384]{3,1,0,2:T(2,128)(2,1)}), bf16[2,2,1024,384]{3,1,0,2:T(2,128)(2,1)}, u32[]{:S(2)}, u32[]{:S(2)}) %all-to-all-start.4) | async-done | bytes 3145760 | tf_op jit(solution)/shard_map/all_to_all | solution.py:117
  774.0 7.1 all-to-all-start.11
  784.9 2.8 copy.217
  787.7 4.6 squeeze.32
  792.3 4.2 copy.218
  796.5 4.7 squeeze.33
  805.0 10.9 %all-to-all-start.5 = ((bf16[64,16,384]{2,1,0:T(8,128)(2,1)}), bf16[64,16,384]{2,1,0:T(8,128)(2,1)}, u32[]{:S(2)}, u32[]{:S(2)}) async-start(bf16[64,16,384]{2,1,0:T(8,128)(2,1)} %copy.219), calls=%async_computation.5 | async-start | bytes 1572864 | tf_op jit(solution)/shard_map/all_to_all | solution.py:118
  820.1 3.0 copy.244
  827.8 10.8 %all-to-all-done.5 = bf16[64,16,384]{2,1,0:T(8,128)(2,1)} async-done(((bf16[64,16,384]{2,1,0:T(8,128)(2,1)}), bf16[64,16,384]{2,1,0:T(8,128)(2,1)}, u32[]{:S(2)}, u32[]{:S(2)}) %all-to-all-start.5) | async-done | bytes 786464 | tf_op jit(solution)/shard_map/all_to_all | solution.py:118
  838.6 5.9 all-to-all-start.9
  844.6 23.0 %all-to-all-done.9 = bf16[64,16,384]{2,1,0:T(8,128)(2,1)S(1)} async-done(((bf16[64,16,384]{2,1,0:T(8,128)(2,1)}), bf16[64,16,384]{2,1,0:T(8,128)(2,1)S(1)}, u32[]{:S(2)}, u32[]{:S(2)}) %all-to-all-start.9) | async-done | bytes 786464 | tf_op jit(solution)/shard_map/all_to_all | solution.py:118
  (153 shorter events, 151.9 us)
Async XLA Ops:
  16.5 13.7 %copy-start.15 = (bf16[1024,384]{1,0:T(8,128)(2,1)S(1)}, bf16[1024,384]{1,0:T(8,128)(2,1)}, u32[]{:S(2)}) copy-start(bf16[1024,384]{1,0:T(8,128)(2,1)} %param.5) | copy-start | bytes 2359300
  16.5 36.6 %all-to-all-start.6 = ((bf16[64,2,3072]{2,1,0:T(2,128)(2,1)}), bf16[64,2,3072]{2,1,0:T(2,128)(2,1)S(1)}, u32[]{:S(2)}, u32[]{:S(2)}) async-start(bf16[64,2,3072]{2,1,0:T(2,128)(2,1)} %reshape.688), calls=%async_computation.6 | async-start | bytes 1572864 | tf_op jit(solution)/shard_map/all_to_all | solution.py:81
  38.0 22.6 %copy-start.14 = (bf16[1,1024,384]{2,1,0:T(8,128)(2,1)S(1)}, bf16[1,1024,384]{2,1,0:T(8,128)(2,1)}, u32[]{:S(2)}) copy-start(bf16[1,1024,384]{2,1,0:T(8,128)(2,1)} %param.4) | copy-start | bytes 2359300
  53.1 29.5 %all-to-all-start.2 = ((bf16[64,2,3072]{2,1,0:T(2,128)(2,1)}), bf16[64,2,3072]{2,1,0:T(2,128)(2,1)}, u32[]{:S(2)}, u32[]{:S(2)}) async-start(bf16[64,2,3072]{2,1,0:T(2,128)(2,1)} %reshape.686), calls=%async_computation.2 | async-start | bytes 1572864 | tf_op jit(solution)/shard_map/all_to_all | solution.py:81
  82.6 29.2 %all-to-all-start = ((bf16[64,2,3072]{2,1,0:T(2,128)(2,1)}), bf16[64,2,3072]{2,1,0:T(2,128)(2,1)}, u32[]{:S(2)}, u32[]{:S(2)}) async-start(bf16[64,2,3072]{2,1,0:T(2,128)(2,1)} %reshape.684), calls=%async_computation | async-start | bytes 1572864 | tf_op jit(solution)/shard_map/all_to_all | solution.py:81
  95.8 1.1 copy-start.10
  117.6 2.4 copy-start.9
  119.3 2.1 copy-start.8
  131.6 78.5 %all-to-all-start.1 = ((bf16[2,128,16,384]{3,2,0,1:T(8,128)(2,1)}), bf16[2,128,16,384]{3,2,0,1:T(8,128)(2,1)S(1)}, u32[]{:S(2)}, u32[]{:S(2)}) async-start(bf16[2,128,16,384]{3,2,0,1:T(8,128)(2,1)} %copy.180), calls=%async_computation.1 | async-start | bytes 6291456 | tf_op jit(solution)/shard_map/all_to_all | solution.py:83
  210.1 1.7 copy-start.3
  211.8 79.4 %all-to-all-start.3 = ((bf16[2,128,16,384]{3,2,0,1:T(8,128)(2,1)}), bf16[2,128,16,384]{3,2,0,1:T(8,128)(2,1)}, u32[]{:S(2)}, u32[]{:S(2)}) async-start(bf16[2,128,16,384]{3,2,0,1:T(8,128)(2,1)} %copy.193), calls=%async_computation.3 | async-start | bytes 6291456 | tf_op jit(solution)/shard_map/all_to_all | solution.py:83
  291.3 79.0 %all-to-all-start.7 = ((bf16[2,128,16,384]{3,2,0,1:T(8,128)(2,1)}), bf16[2,128,16,384]{3,2,0,1:T(8,128)(2,1)S(1)}, u32[]{:S(2)}, u32[]{:S(2)}) async-start(bf16[2,128,16,384]{3,2,0,1:T(8,128)(2,1)} %copy.223), calls=%async_computation.7 | async-start | bytes 6291456 | tf_op jit(solution)/shard_map/all_to_all | solution.py:83
  297.9 185.0 %all-reduce.2.cloned.1.call-start = ((), (), s32[]{:S(2)}) async-start(), calls=%async_computation.12 | async-start | bytes 6291456 | tf_op jit(solution)/shard_map/psum | solution.py:148
  372.7 2.5 copy-start.6
  372.7 4.0 copy-start.7
  405.1 2.2 copy-start.1
  410.8 2.3 copy-start
  489.0 2.5 copy-start.2
  489.0 4.0 copy-start.4
  530.0 83.3 %all-to-all-start.10 = ((bf16[2,2,1024,384]{3,1,0,2:T(2,128)(2,1)}), bf16[2,2,1024,384]{3,1,0,2:T(2,128)(2,1)S(1)}, u32[]{:S(2)}, u32[]{:S(2)}) async-start(bf16[2,2,1024,384]{3,1,0,2:T(2,128)(2,1)} %copy.258), calls=%async_computation.10 | async-start | bytes 6291456 | tf_op jit(solution)/shard_map/all_to_all | solution.py:117
  613.3 1.7 copy-start.5
  615.0 79.1 %all-to-all-start.8 = ((bf16[2,2,1024,384]{3,1,0,2:T(2,128)(2,1)}), bf16[2,2,1024,384]{3,1,0,2:T(2,128)(2,1)S(1)}, u32[]{:S(2)}, u32[]{:S(2)}) async-start(bf16[2,2,1024,384]{3,1,0,2:T(2,128)(2,1)} %copy.241), calls=%async_computation.8 | async-start | bytes 6291456 | tf_op jit(solution)/shard_map/all_to_all | solution.py:117
  694.2 79.9 %all-to-all-start.4 = ((bf16[2,2,1024,384]{3,1,0,2:T(2,128)(2,1)}), bf16[2,2,1024,384]{3,1,0,2:T(2,128)(2,1)}, u32[]{:S(2)}, u32[]{:S(2)}) async-start(bf16[2,2,1024,384]{3,1,0,2:T(2,128)(2,1)} %copy.215), calls=%async_computation.4 | async-start | bytes 6291456 | tf_op jit(solution)/shard_map/all_to_all | solution.py:117
  721.7 2.0 copy-start.11
  774.0 31.0 %all-to-all-start.11 = ((bf16[64,16,384]{2,1,0:T(8,128)(2,1)}), bf16[64,16,384]{2,1,0:T(8,128)(2,1)}, u32[]{:S(2)}, u32[]{:S(2)}) async-start(bf16[64,16,384]{2,1,0:T(8,128)(2,1)} %copy.262), calls=%async_computation.11 | async-start | bytes 1572864 | tf_op jit(solution)/shard_map/all_to_all | solution.py:118
  801.2 2.0 copy-start.12
  805.0 33.6 %all-to-all-start.5 = ((bf16[64,16,384]{2,1,0:T(8,128)(2,1)}), bf16[64,16,384]{2,1,0:T(8,128)(2,1)}, u32[]{:S(2)}, u32[]{:S(2)}) async-start(bf16[64,16,384]{2,1,0:T(8,128)(2,1)} %copy.219), calls=%async_computation.5 | async-start | bytes 1572864 | tf_op jit(solution)/shard_map/all_to_all | solution.py:118
  824.6 1.4 copy-start.13
  838.6 28.9 %all-to-all-start.9 = ((bf16[64,16,384]{2,1,0:T(8,128)(2,1)}), bf16[64,16,384]{2,1,0:T(8,128)(2,1)S(1)}, u32[]{:S(2)}, u32[]{:S(2)}) async-start(bf16[64,16,384]{2,1,0:T(8,128)(2,1)} %copy.245), calls=%async_computation.9 | async-start | bytes 1572864 | tf_op jit(solution)/shard_map/all_to_all | solution.py:118
Sparse Core Ops, SparseCore 0:
  404.8 77.9 all-reduce.1
where the time goes:
time: 888 us; the launch traced here: 880 us
  waiting for transfers between devices  501 us (56%)
  local copies, waits for them, and re-layouts  135 us (15%)
  matrix products  97.2 us (11%)
  starting transfers between devices  95.9 us (11%)
  other arithmetic  35.6 us (4%)
  between operations  15.6 us (2%)
    all_to_all x3, waiting for transfers between devices, forward(): lax.all_to_all(spread, 'seq', split_axis=1, concat_axis=2, tiled=True)  187 us
    all_to_all x3, waiting for transfers between devices, inverse(): lax.all_to_all(packed, 'seq', split_axis=2, concat_axis=1, tiled=True)  179 us
    psum x1, waiting for transfers between devices, per_device(): lax.psum(spec_weight.astype(jnp.bfloat16), 'dp').astype(jnp.float32)  65.2 us
    all_to_all x3, waiting for transfers between devices, forward(): lax.all_to_all(values, 'seq', split_axis=1, concat_axis=0, tiled=True)  36 us
    unnamed x45, local copies, waits for them, and re-layouts  34.1 us
    all_to_all x3, waiting for transfers between devices, inverse(): lax.all_to_all(columns, 'seq', split_axis=0, concat_axis=1, tiled=True)  33.8 us
    all_to_all x3, starting transfers between devices, forward(): lax.all_to_all(values, 'seq', split_axis=1, concat_axis=0, tiled=True)  26.9 us
    all_to_all x3, starting transfers between devices, inverse(): lax.all_to_all(packed, 'seq', split_axis=2, concat_axis=1, tiled=True)  25 us
  transfers between devices with their start and end apart: 13, of which 12 were waited for; matrix products, arithmetic and copies ran while one was open for 17% of the time, Pallas kernels for 0%

commit v1 on v0

v1 whole, which is shorter than its diff:
```python
import functools
import math

import jax
import jax.numpy as jnp
import numpy as np
from jax import lax
from jax.experimental import pallas as pl
from jax.experimental.pallas import tpu as pltpu
from jax.sharding import PartitionSpec as P

LANES = 128
ROWS = 8
SLICES = 3
PAD = 16


def make_tables(all_rows):
    full = 2 * all_rows
    period = full * LANES
    kept = all_rows + 1
    height = -(-kept // (SLICES * PAD)) * PAD
    ids = np.arange(SLICES * height)
    valid = (ids < kept).astype(np.float64)
    outer = 2.0 * np.pi / full * ((ids[:, None] * np.arange(all_rows)[None, :]) % full)
    cos_outer = (np.cos(outer) * valid[:, None]).reshape(SLICES, height, all_rows)
    sin_outer = (np.sin(outer) * valid[:, None]).reshape(SLICES, height, all_rows)
    first = np.concatenate([cos_outer, -sin_outer], axis=1)
    turn = 2.0 * np.pi / period * ((ids[:, None] * np.arange(LANES)[None, :]) % period)
    twist = np.stack([np.cos(turn), np.sin(turn)]).reshape(2, SLICES, height, LANES)
    weight = np.where((ids == 0) | (ids == all_rows), 1.0, 2.0) * valid
    back = np.concatenate([cos_outer, -sin_outer], axis=1)
    back = back * np.concatenate([weight.reshape(SLICES, height, 1)] * 2, axis=1)
    back = back.reshape(SLICES * 2 * height, all_rows).T
    inner = 2.0 * np.pi / LANES * ((np.arange(LANES)[:, None] * np.arange(LANES)[None, :]) % LANES)
    cos_in, sin_in = np.cos(inner), np.sin(inner)
    forward_in = np.block([[cos_in, -sin_in], [sin_in, cos_in]])
    inverse_in = np.block([[cos_in, sin_in], [-sin_in, cos_in]])
    low = lambda table: jnp.asarray(table.astype(np.float32), jnp.bfloat16)
    return (
        low(first),
        jnp.asarray(twist.astype(np.float32)),
        low(forward_in),
        low(inverse_in),
        low(back),
    )


def dot(left, right):
    return jnp.dot(left, right, preferred_element_type=jnp.float32)


def turn_over(left, right):
    return lax.dot_general(left, right, (((1,), (1,)), ((), ())), preferred_element_type=jnp.float32)


def gather_body(mask_ref, unit_ref, sig_ref, cot_ref, fil_ref, pair_ref, solo_ref, hold):
    unit = unit_ref[...]

    def flipped(ref):
        out = turn_over(unit, ref[...])
        for row in range(ROWS):
            hold[pl.ds(row, LANES, stride=ROWS), :] = out[:, row * LANES : (row + 1) * LANES]
        return hold[...].reshape(LANES, ROWS, LANES)

    keep = mask_ref[0, 0].astype(jnp.float32)
    pair_ref[:, :ROWS, :] = (flipped(sig_ref) * keep).astype(jnp.bfloat16)
    pair_ref[:, ROWS:, :] = flipped(cot_ref).astype(jnp.bfloat16)
    solo_ref[...] = flipped(fil_ref).astype(jnp.bfloat16)


def to_channels(block_mask, unit, signal, cotangent, filter_raw):
    tokens, channels = filter_raw.shape
    column = pl.BlockSpec((tokens, LANES), lambda i: (0, i))
    return pl.pallas_call(
        gather_body,
        grid=(channels // LANES,),
        in_specs=[
            pl.BlockSpec(memory_space=pltpu.SMEM),
            pl.BlockSpec((LANES, LANES), lambda i: (0, 0)),
            column,
            column,
            column,
        ],
        out_specs=[
            pl.BlockSpec((LANES, 2 * ROWS, LANES), lambda i: (i, 0, 0)),
            pl.BlockSpec((LANES, ROWS, LANES), lambda i: (i, 0, 0)),
        ],
        out_shape=[
            jax.ShapeDtypeStruct((channels, 2 * ROWS, LANES), jnp.bfloat16),
            jax.ShapeDtypeStruct((channels, ROWS, LANES), jnp.bfloat16),
        ],
        scratch_shapes=[pltpu.VMEM((LANES * ROWS, LANES), jnp.float32)],
        name="to_channels",
    )(block_mask, unit, signal, cotangent, filter_raw)


def scatter_body(mask_ref, unit_ref, pair_ref, solo_ref, out_ref, grad_ref, fil_ref, hold, lone):
    unit = unit_ref[...]
    hold[...] = pair_ref[...].astype(jnp.float32).reshape(LANES * 2 * ROWS, LANES)
    lone[...] = solo_ref[...].astype(jnp.float32).reshape(LANES * ROWS, LANES)
    keep = mask_ref[0, 0].astype(jnp.float32)

    def turned(ref, start, stride):
        rows = ref[pl.ds(start, LANES, stride=stride), :].astype(jnp.bfloat16)
        return turn_over(unit, rows)

    for row in range(ROWS):
        here = slice(row * LANES, (row + 1) * LANES)
        out_ref[here, :] = turned(hold, row, 2 * ROWS).astype(jnp.bfloat16)
        grad_ref[here, :] = (turned(hold, ROWS + row, 2 * ROWS) * keep).astype(jnp.bfloat16)
        fil_ref[here, :] = turned(lone, row, ROWS).astype(jnp.bfloat16)


def to_tokens(block_mask, unit, pair, solo):
    channels = solo.shape[0]
    tokens = ROWS * LANES
    column = pl.BlockSpec((tokens, LANES), lambda i: (0, i))
    return pl.pallas_call(
        scatter_body,
        grid=(channels // LANES,),
        in_specs=[
            pl.BlockSpec(memory_space=pltpu.SMEM),
            pl.BlockSpec((LANES, LANES), lambda i: (0, 0)),
            pl.BlockSpec((LANES, 2 * ROWS, LANES), lambda i: (i, 0, 0)),
            pl.BlockSpec((LANES, ROWS, LANES), lambda i: (i, 0, 0)),
        ],
        out_specs=[column, column, column],
        out_shape=[jax.ShapeDtypeStruct((tokens, channels), jnp.bfloat16)] * 3,
        scratch_shapes=[
            pltpu.VMEM((LANES * 2 * ROWS, LANES), jnp.float32),
            pltpu.VMEM((LANES * ROWS, LANES), jnp.float32),
        ],
        name="to_tokens",
    )(block_mask, unit, pair, solo)


def lane(index):
    return slice(index * LANES, (index + 1) * LANES)


def forward_slice(step, columns, rows_ref, first_ref, twist_ref, inner_ref):
    height = twist_ref.shape[2]
    cos, sin = twist_ref[0, step], twist_ref[1, step]
    mixed = dot(first_ref[step], rows_ref[...])
    spectra = []
    for column in range(columns):
        real, imag = mixed[:height, lane(column)], mixed[height:, lane(column)]
        turned = jnp.concatenate([real * cos + imag * sin, imag * cos - real * sin], axis=1)
        spectra.append(dot(turned.astype(jnp.bfloat16), inner_ref[...]))
    return spectra


def split(pair):
    return pair[:, :LANES], pair[:, LANES:]


def filter_spectrum(count, rows_ref, spec_ref, first_ref, twist_ref, inner_ref):
    def step_body(step, carry):
        spectra = forward_slice(step, count, rows_ref, first_ref, twist_ref, inner_ref)
        for index, spectrum in enumerate(spectra):
            spec_ref[index, step] = spectrum
        return carry

    lax.fori_loop(0, SLICES, step_body, 0)


def convolve(count, rows_ref, spec_ref, back_rows, tables):
    first_ref, twist_ref, inner_ref, outer_ref = tables
    height = twist_ref.shape[2]

    def step_body(step, carry):
        spectra = forward_slice(step, 2 * count, rows_ref, first_ref, twist_ref, inner_ref)
        cos, sin = twist_ref[0, step], twist_ref[1, step]
        for index in range(count):
            sig_r, sig_i = split(spectra[index])
            cot_r, cot_i = split(spectra[count + index])
            fil_r, fil_i = split(spec_ref[index, step])
            products = (
                (sig_r * fil_r - sig_i * fil_i, sig_r * fil_i + sig_i * fil_r),
                (cot_r * fil_r + cot_i * fil_i, cot_i * fil_r - cot_r * fil_i),
                (cot_r * sig_r + cot_i * sig_i, cot_i * sig_r - cot_r * sig_i),
            )
            for which, product in enumerate(products):
                low = jnp.concatenate(product, axis=1).astype(jnp.bfloat16)
                real, imag = split(dot(low, outer_ref[...]))
                column = lane(3 * index + which)
                back_rows[step, :height, column] = (real * cos - imag * sin).astype(jnp.bfloat16)
                back_rows[step, height:, column] = (imag * cos + real * sin).astype(jnp.bfloat16)
        return carry

    lax.fori_loop(0, SLICES, step_body, 0)


def finish(index, factor, back_rows, back_ref):
    depth = back_ref.shape[1]
    columns = slice(3 * index * LANES, 3 * (index + 1) * LANES)
    result = dot(back_ref[...], back_rows[:, :, columns].reshape(depth, 3 * LANES)) * factor
    blocks = result.shape[0] // ROWS
    return [result[:, lane(which)].reshape(blocks, ROWS, LANES) for which in range(3)]


LONG = 8
SHORT = 4
CORES = 2
HALVES = 2


def zigzag(step):
    return LONG + lax.div(step + 1, 2) * (1 - 2 * lax.rem(step, 2))


def partner(place, step):
    mixed = lax.rem(step * 27, LONG * SHORT * CORES)
    z = lax.rem(lax.div(place, SHORT * CORES) + zigzag(lax.rem(mixed, LONG)), LONG)
    y = lax.rem(lax.div(place, CORES) + lax.div(mixed, LONG), SHORT)
    core = lax.rem(place + lax.div(mixed, LONG * SHORT), CORES)
    return (z * SHORT + y) * CORES + core


def partner_chip(place, step):
    mixed = lax.rem(step * 11, LONG * SHORT)
    z = lax.rem(lax.div(place, SHORT * CORES) + zigzag(lax.rem(mixed, LONG)), LONG)
    y = lax.rem(lax.div(place, CORES) + lax.div(mixed, LONG), SHORT)
    return z * SHORT + y


def exchange_body(factor, pair_ref, solo_ref, *refs):
    table_refs, refs = refs[:5], refs[5:]
    pair_out, fil_out = refs[:2]
    tables = refs[2:7]
    pair_in, fil_in, rows, fil_rows, spec, back_rows, pair_done, part, parts, summed = refs[7:17]
    (table_sem, pair_sem, fil_sem, out_sem, part_sem, piece_sem, share_sem, sent_pair, sent_fil, sent_near,
     sent_fil_dp, sent_part, sent_out, sent_piece, sent_share) = refs[17:]
    peers, _, count = pair_ref.shape[:3]
    replicas = lax.axis_size("dp")
    place = lax.axis_index("seq")
    replica = lax.axis_index("dp")
    chip, core = lax.div(place, CORES), lax.rem(place, CORES)
    own_core, own_half = lax.div(replica, HALVES), lax.rem(replica, HALVES)
    sharer = core == own_core

    def remote(source, target, sent, received, **where):
        return pltpu.make_async_remote_copy(
            src_ref=source, dst_ref=target, send_sem=sent, recv_sem=received,
            device_id=where, device_id_type=pl.DeviceIdType.MESH,
        )

    def settle(like, sem):
        pltpu.make_async_copy(like, like, sem).wait()

    loads = [
        pltpu.make_async_copy(source, target, table_sem.at[index])
        for index, (source, target) in enumerate(zip(table_refs, tables))
    ]
    for load in loads:
        load.start()

    barrier = pltpu.get_barrier_semaphore()

    def greet(step, carry):
        pl.semaphore_signal(
            barrier, 1, device_id={"seq": partner(place, step)}, device_id_type=pl.DeviceIdType.MESH
        )
        return carry

    def greet_replica(step, carry):
        pl.semaphore_signal(
            barrier, 1, device_id={"dp": lax.rem(replica + step, replicas)}, device_id_type=pl.DeviceIdType.MESH
        )
        return carry

    lax.fori_loop(1, peers, greet, 0)
    lax.fori_loop(1, replicas, greet_replica, 0)
    pl.semaphore_wait(barrier, peers - 1 + replicas - 1)

    def filter_copy(to_chip):
        to = to_chip * CORES + own_core
        return remote(
            solo_ref.at[to, own_half], fil_in.at[own_half, place], sent_fil, fil_sem.at[own_half], seq=to
        )

    def near_copy():
        to = chip * CORES + own_core
        return remote(
            solo_ref.at[to, own_half], fil_in.at[own_half, place], sent_near, fil_sem.at[own_half], seq=to
        )

    def send_filter(step, carry):
        filter_copy(partner_chip(place, step)).start()
        return carry

    lax.fori_loop(1, peers // CORES, send_filter, 0)

    @pl.when(sharer)
    def _():
        pltpu.make_async_copy(
            solo_ref.at[place, own_half], fil_in.at[own_half, place], fil_sem.at[own_half]
        ).start()

    @pl.when(jnp.logical_not(sharer))
    def _():
        near_copy().start()

    def send_pairs(half):
        pltpu.make_async_copy(pair_ref.at[place, half], pair_in.at[half, place], pair_sem.at[half]).start()

        def send(step, carry):
            to = partner(place, step)
            remote(
                pair_ref.at[to, half], pair_in.at[half, place], sent_pair, pair_sem.at[half], seq=to
            ).start()
            return carry

        lax.fori_loop(1, peers, send, 0)

    send_pairs(0)

    @pl.when(sharer)
    def _():
        settle(fil_in.at[own_half], fil_sem.at[own_half])

        def share(step, carry):
            remote(
                fil_in.at[own_half], fil_in.at[own_half], sent_fil_dp, fil_sem.at[own_half],
                dp=lax.rem(replica + step, replicas),
            ).start()
            return carry

        lax.fori_loop(1, replicas, share, 0)

    send_pairs(1)

    for half in range(HALVES):
        @pl.when(replica != core * HALVES + half)
        def _():
            settle(fil_in.at[half], fil_sem.at[half])

    for load in loads:
        load.wait()
    first_ref, twist_ref, inner_ref, outer_ref, back_ref = tables
    height = peers * ROWS
    for half in range(HALVES):
        for index in range(count):
            alone = fil_in[half, :, index].astype(jnp.float32)
            fil_rows[:, lane(index)] = alone.reshape(height, LANES).astype(jnp.bfloat16)
        filter_spectrum(count, fil_rows, spec.at[half], first_ref, twist_ref, inner_ref)

    def transform(half):
        for index in range(count):
            both = pair_in[half, :, index].astype(jnp.float32)
            rows[:, lane(index)] = both[:, :ROWS].reshape(height, LANES).astype(jnp.bfloat16)
            rows[:, lane(count + index)] = both[:, ROWS:].reshape(height, LANES).astype(jnp.bfloat16)
        convolve(count, rows, spec.at[half], back_rows, (first_ref, twist_ref, inner_ref, outer_ref))
        for index in range(count):
            conv, grad, weight = finish(index, factor, back_rows, back_ref)
            pair_done[half, :, index] = jnp.concatenate([conv, grad], axis=1).astype(jnp.bfloat16)
            part[half, :, index] = weight.astype(jnp.bfloat16)

    def send_part(half):
        owner = core * HALVES + half

        @pl.when(replica != owner)
        def _():
            slot = lax.rem(replica - owner + replicas, replicas) - 1
            remote(part.at[half], parts.at[slot], sent_part.at[half], part_sem, dp=owner).start()

    def send_done(half):
        pltpu.make_async_copy(pair_done.at[half, place], pair_out.at[place, half], out_sem).start()

        def send(step, carry):
            to = partner(place, step)
            remote(pair_done.at[half, to], pair_out.at[place, half], sent_out, out_sem, seq=to).start()
            return carry

        lax.fori_loop(1, peers, send, 0)

    def collect(half):
        @pl.when(replica == core * HALVES + half)
        def _():
            settle(parts, part_sem)

            def add(block, carry):
                here = pl.ds(block * ROWS, ROWS)
                total = part[half, here].astype(jnp.float32)
                for slot in range(parts.shape[0]):
                    total = total + parts[slot, here].astype(jnp.float32)
                summed[here] = total.astype(jnp.bfloat16)
                return carry

            lax.fori_loop(0, peers // ROWS, add, 0)
            pltpu.make_async_copy(summed.at[place], fil_out.at[chip, replica], piece_sem).start()

            def send(step, carry):
                to = partner(place, step)
                remote(summed.at[to], fil_out.at[chip, replica], sent_piece, piece_sem, seq=to).start()
                return carry

            lax.fori_loop(1, peers, send, 0)

    settle(pair_in.at[0], pair_sem.at[0])
    transform(0)
    send_part(0)
    send_done(0)
    settle(pair_in.at[1], pair_sem.at[1])
    collect(0)
    transform(1)
    send_part(1)
    collect(1)
    send_done(1)

    settle(summed.at[pl.ds(0, peers // CORES)], piece_sem)

    def share_sum(step, carry):
        remote(
            fil_out.at[:, replica], fil_out.at[:, replica], sent_share, share_sem,
            dp=lax.rem(replica + step, replicas),
        ).start()
        return carry

    lax.fori_loop(1, replicas, share_sum, 0)
    shares = fil_out.at[pl.ds(0, (replicas - 1) * peers // CORES // replicas)]
    settle(shares, share_sem)
    settle(pair_out, out_sem)
    settle(pair_ref.at[pl.ds(0, peers - 1)], sent_pair)
    settle(solo_ref.at[pl.ds(0, peers // CORES - 1), 0], sent_fil)

    @pl.when(sharer)
    def _():
        settle(parts, sent_fil_dp)
        settle(summed.at[pl.ds(0, peers - 1)], sent_piece)

    @pl.when(jnp.logical_not(sharer))
    def _():
        settle(summed.at[0], sent_near)

    for half in range(HALVES):
        @pl.when(replica != core * HALVES + half)
        def _():
            settle(part.at[half], sent_part.at[half])

    settle(pair_done.at[:, pl.ds(0, peers - 1)], sent_out)
    settle(shares, sent_share)


def exchange(pair, solo, tables, factor):
    peers, halves, count = pair.shape[:3]
    height = tables[1].shape[2]
    replicas = lax.axis_size("dp")
    whole = pl.BlockSpec(memory_space=pltpu.VMEM)
    anywhere = pl.BlockSpec(memory_space=pl.ANY)
    low = jnp.bfloat16
    tile, half_tile = (count, 2 * ROWS, LANES), (count, ROWS, LANES)
    dma = pltpu.SemaphoreType.DMA
    return pl.pallas_call(
        functools.partial(exchange_body, factor),
        in_specs=[anywhere] * 7,
        out_specs=[whole] * 2,
        out_shape=[
            jax.ShapeDtypeStruct(pair.shape, low),
            jax.ShapeDtypeStruct((peers // CORES, CORES * HALVES) + half_tile, low),
        ],
        scratch_shapes=[pltpu.VMEM(table.shape, table.dtype) for table in tables]
        + [
            pltpu.VMEM((halves, peers) + tile, low),
            pltpu.VMEM((halves, peers) + half_tile, low),
            pltpu.VMEM((peers * ROWS, 2 * count * LANES), low),
            pltpu.VMEM((peers * ROWS, count * LANES), low),
            pltpu.VMEM((halves, count, SLICES, height, 2 * LANES), jnp.float32),
            pltpu.VMEM((SLICES, 2 * height, 3 * count * LANES), low),
            pltpu.VMEM((halves, peers) + tile, low),
            pltpu.VMEM((halves, peers) + half_tile, low),
            pltpu.VMEM((replicas - 1, peers) + half_tile, low),
            pltpu.VMEM((peers,) + half_tile, low),
        ]
        + [dma((len(tables),)), dma((halves,)), dma((halves,)), dma, dma, dma, dma, dma, dma, dma, dma,
           dma((halves,)), dma, dma, dma],
        compiler_params=pltpu.CompilerParams(collective_id=0, has_side_effects=True),
        name="exchange",
    )(pair, solo, *tables)


def per_device(signal, filter_raw, cotangent, block_mask):
    tokens, channels = filter_raw.shape
    peers = lax.axis_size("seq")
    own = channels // peers
    tables = make_tables(peers * tokens // LANES)
    total = peers * tokens
    factor = 1.0 / (2 * total * math.sqrt(total))
    unit = jnp.asarray(np.eye(LANES, dtype=np.float32), jnp.bfloat16)
    pair, solo = to_channels(block_mask, unit, signal[0], cotangent[0], filter_raw)
    count = own // HALVES
    pair, solo = exchange(
        pair.reshape(peers, HALVES, count, 2 * ROWS, LANES),
        solo.reshape(peers, HALVES, count, ROWS, LANES),
        tables,
        factor,
    )
    conv, grad, weight = to_tokens(
        block_mask, unit, pair.reshape(channels, 2 * ROWS, LANES), solo.reshape(channels, ROWS, LANES)
    )
    return conv[None], grad[None], weight


def solution(mesh):
    placed = (P("dp", "seq", None), P("seq", None), P("dp", "seq", None), P("dp", "seq"))
    return jax.shard_map(
        per_device,
        mesh=mesh,
        in_specs=placed,
        out_specs=(P("dp", "seq", None), P("dp", "seq", None), P("seq", None)),
        check_vma=False,
    )
```

time: 888 us -> 106 us (0.12)
  waiting for transfers between devices: 501 us -> 0 us
  local copies, waits for them, and re-layouts: 135 us -> 0 us
  Pallas kernels: 0 us -> 105 us
  matrix products: 97.2 us -> 0 us
  starting transfers between devices: 95.9 us -> 0 us
  other arithmetic: 35.6 us -> 0 us
  between operations: 15.6 us -> 1.29 us
    all_to_all x12 -> x0, waiting for transfers between devices: 436 us -> none  [the longest x3 187 us: forward(): lax.all_to_all(spread, 'seq', split_axis=1, concat_axis=2, tiled=True)]
    pallas_call x0 -> x3, Pallas kernels: none -> 105 us  [the longest x1 95.3 us: exchange(): pl.pallas_call(functools.partial(exchange_body, factor), in_specs=[anywhe...]
    dot_general x60 -> x0, matrix products: 97.2 us -> none  [the longest x3 11.5 us: inverse(): jnp.einsum('sq,ksrc->krqc', sin_rad, rounded_spec[1], preferred_element_t...]
    all_to_all x12 -> x0, starting transfers between devices: 95.5 us -> none  [the longest x3 26.9 us: forward(): lax.all_to_all(values, 'seq', split_axis=1, concat_axis=0, tiled=True)]
    psum x1 -> x0, waiting for transfers between devices: 65.2 us -> none  [per_device(): lax.psum(spec_weight.astype(jnp.bfloat16), 'dp').astype(jnp.float32)]
    unnamed x45 -> x0, local copies, waits for them, and re-layouts: 34.1 us -> none
    slice x19 -> x0, local copies, waits for them, and re-layouts: 27.2 us -> none  [the longest x6 15.9 us: outer_back(): portion[1]]
    another operation x6 -> x0, local copies, waits for them, and re-layouts: 25.3 us -> none  [the longest x3 14.7 us: inverse(): packed = jnp.stack([turned_real, turned_imag]).astype(jnp.bfloat16)]
  transfers between devices with their start and end apart: 13 -> 0, of which waited for: 12 -> 0; matrix products, arithmetic and copies ran while one was open for 17% -> 0% of each run, Pallas kernels for 0% -> 0%
where the time goes in v1:
time: 106 us
  Pallas kernels  105 us (99%)
  between operations  1.29 us (1%)
    pallas_call x1, Pallas kernels, exchange(): pl.pallas_call(functools.partial(exchange_body, factor), in_specs=[anywhe...  95.3 us
    pallas_call x1, Pallas kernels, to_tokens(): pl.pallas_call(scatter_body, grid=(channels // LANES,), in_specs=[pl.Bloc...  4.9 us
    pallas_call x1, Pallas kernels, to_channels(): pl.pallas_call(gather_body, grid=(channels // LANES,), in_specs=[pl.Block...  4.34 us

profile of v1, /device:TPU:1, one launch (start us, length us, event | category | flops | bytes accessed | tf_op | source)
XLA Modules:
  0.0 105.8 jit_solution(3003740426073548390)
XLA Ops:
  1.3 4.3 %to_channels.1 = (bf16[384,16,128]{2,1,0:T(8,128)(2,1)}, bf16[384,8,128]{2,1,0:T(8,128)(2,1)}) custom-call(s32[1,1]{1,0:T(1,128)S(6)} %copy.13.mask_ref, bf16[128,128]{1,0:T(8,128)(2,1)} %constant.17.clone.unit_ref, bf16[1024,384]{1,0:T(8,128)(2,1)} %bitcast.10, bf16[1024,384]{1,0:T(8,128)(2,1)} %bitcast.11, bf16[1024,384]{1,0:T(8,128)(2,1)} %fil_ref.1), custom_call_target="tpu_custom_call" | custom-call | tf_op jit(solution)/shard_map/to_channels/pallas_call | solution.py:75
  5.6 95.3 %exchange.1 = (bf16[64,2,3,16,128]{4,3,2,1,0:T(8,128)(2,1)}, bf16[32,4,3,8,128]{4,3,2,1,0:T(8,128)(2,1)}) custom-call(bf16[64,2,3,16,128]{4,3,2,1,0:T(8,128)(2,1)} %bitcast.9, bf16[64,2,3,8,128]{4,3,2,1,0:T(8,128)(2,1)} %bitcast.13, bf16[3,352,512]{2,1,0:T(8,128)(2,1)} %constant.12.clone.refs_0_, f32[2,3,176,128]{3,2,1,0:T(8,128)} %constant.13.clone.refs_1_, ...), custom_call_target="tpu_custom_call" | custom-call | tf_op jit(solution)/shard_map/exchange/pallas_call | solution.py:455
  100.9 4.9 %to_tokens.1 = (bf16[1024,384]{1,0:T(8,128)(2,1)}, bf16[1024,384]{1,0:T(8,128)(2,1)}, bf16[1024,384]{1,0:T(8,128)(2,1)}) custom-call(s32[1,1]{1,0:T(1,128)S(6)} %copy.13.mask_ref, bf16[128,128]{1,0:T(8,128)(2,1)} %constant.17.clone.unit_ref, bf16[384,16,128]{2,1,0:T(8,128)(2,1)} %bitcast.8, bf16[384,8,128]{2,1,0:T(8,128)(2,1)} %bitcast.12), custom_call_target="tpu_custom_call" | custom-call | tf_op jit(solution)/shard_map/to_tokens/pallas_call | solution.py:119

commit v2 on v1

--- a/solution.py
+++ b/solution.py
@@ -54,47 +54,6 @@
     return lax.dot_general(left, right, (((1,), (1,)), ((), ())), preferred_element_type=jnp.float32)
 
 
-def gather_body(mask_ref, unit_ref, sig_ref, cot_ref, fil_ref, pair_ref, solo_ref, hold):
-    unit = unit_ref[...]
-
-    def flipped(ref):
-        out = turn_over(unit, ref[...])
-        for row in range(ROWS):
-            hold[pl.ds(row, LANES, stride=ROWS), :] = out[:, row * LANES : (row + 1) * LANES]
-        return hold[...].reshape(LANES, ROWS, LANES)
-
-    keep = mask_ref[0, 0].astype(jnp.float32)
-    pair_ref[:, :ROWS, :] = (flipped(sig_ref) * keep).astype(jnp.bfloat16)
-    pair_ref[:, ROWS:, :] = flipped(cot_ref).astype(jnp.bfloat16)
-    solo_ref[...] = flipped(fil_ref).astype(jnp.bfloat16)
-
-
-def to_channels(block_mask, unit, signal, cotangent, filter_raw):
-    tokens, channels = filter_raw.shape
-    column = pl.BlockSpec((tokens, LANES), lambda i: (0, i))
-    return pl.pallas_call(
-        gather_body,
-        grid=(channels // LANES,),
-        in_specs=[
-            pl.BlockSpec(memory_space=pltpu.SMEM),
-            pl.BlockSpec((LANES, LANES), lambda i: (0, 0)),
-            column,
-            column,
-            column,
-        ],
-        out_specs=[
-            pl.BlockSpec((LANES, 2 * ROWS, LANES), lambda i: (i, 0, 0)),
-            pl.BlockSpec((LANES, ROWS, LANES), lambda i: (i, 0, 0)),
-        ],
-        out_shape=[
-            jax.ShapeDtypeStruct((channels, 2 * ROWS, LANES), jnp.bfloat16),
-            jax.ShapeDtypeStruct((channels, ROWS, LANES), jnp.bfloat16),
-        ],
-        scratch_shapes=[pltpu.VMEM((LANES * ROWS, LANES), jnp.float32)],
-        name="to_channels",
-    )(block_mask, unit, signal, cotangent, filter_raw)
-
-
 def scatter_body(mask_ref, unit_ref, pair_ref, solo_ref, out_ref, grad_ref, fil_ref, hold, lone):
     unit = unit_ref[...]
     hold[...] = pair_ref[...].astype(jnp.float32).reshape(LANES * 2 * ROWS, LANES)
@@ -206,33 +165,73 @@
 HALVES = 2
 
 
-def zigzag(step):
-    return LONG + lax.div(step + 1, 2) * (1 - 2 * lax.rem(step, 2))
-
-
-def partner(place, step):
-    mixed = lax.rem(step * 27, LONG * SHORT * CORES)
-    z = lax.rem(lax.div(place, SHORT * CORES) + zigzag(lax.rem(mixed, LONG)), LONG)
-    y = lax.rem(lax.div(place, CORES) + lax.div(mixed, LONG), SHORT)
-    core = lax.rem(place + lax.div(mixed, LONG * SHORT), CORES)
-    return (z * SHORT + y) * CORES + core
-
-
-def partner_chip(place, step):
-    mixed = lax.rem(step * 11, LONG * SHORT)
-    z = lax.rem(lax.div(place, SHORT * CORES) + zigzag(lax.rem(mixed, LONG)), LONG)
-    y = lax.rem(lax.div(place, CORES) + lax.div(mixed, LONG), SHORT)
-    return z * SHORT + y
-
-
-def exchange_body(factor, pair_ref, solo_ref, *refs):
-    table_refs, refs = refs[:5], refs[5:]
+ZIGZAG = (0, -1, 1, -2, 2, -3, 3, -4)
+
+
+def wrap(value, size):
+    return jnp.where(value >= size, value - size, value)
+
+
+def each_partner(place, visit):
+    z, y, core = lax.div(place, SHORT * CORES), lax.rem(lax.div(place, CORES), SHORT), lax.rem(place, CORES)
+    bases = [wrap(z + shift % LONG, LONG) * (SHORT * CORES) for shift in ZIGZAG]
+    sides = (core, 1 - core)
+
+    def body(turn, carry):
+        first = wrap(y + turn, SHORT)
+        rows = [wrap(first + shift, SHORT) * CORES for shift in range(SHORT)]
+        for swap in range(CORES):
+            for index, base in enumerate(bases):
+                to = base + rows[index % SHORT] + sides[(swap + index // SHORT) % CORES]
+                if swap == 0 and index == 0:
+
+                    @pl.when(turn > 0)
+                    def _():
+                        visit(to)
+                else:
+                    visit(to)
+        return carry
+
+    lax.fori_loop(0, SHORT, body, 0)
+
+
+def each_chip(place, visit):
+    z, y = lax.div(place, SHORT * CORES), lax.rem(lax.div(place, CORES), SHORT)
+    bases = [wrap(z + shift % LONG, LONG) * SHORT for shift in ZIGZAG]
+
+    def body(turn, carry):
+        first = wrap(y + turn, SHORT)
+        rows = [wrap(first + shift, SHORT) for shift in range(SHORT)]
+        for index, base in enumerate(bases):
+            to = base + rows[index % SHORT]
+            if index == 0:
+
+                @pl.when(turn > 0)
+                def _():
+                    visit(to)
+            else:
+                visit(to)
+        return carry
+
+    lax.fori_loop(0, SHORT, body, 0)
+
+
+def flip(unit, tokens_ref, column, hold):
+    across = turn_over(unit, tokens_ref[:, lane(column)])
+    for row in range(ROWS):
+        hold[pl.ds(row, LANES, stride=ROWS), :] = across[:, lane(row)]
+    return hold[...].reshape(LANES, ROWS, LANES)
+
+
+def exchange_body(factor, count, mask_ref, unit_ref, *refs):
+    token_refs, table_refs, refs = refs[:3], refs[3:8], refs[8:]
     pair_out, fil_out = refs[:2]
     tables = refs[2:7]
-    pair_in, fil_in, rows, fil_rows, spec, back_rows, pair_done, part, parts, summed = refs[7:17]
-    (table_sem, pair_sem, fil_sem, out_sem, part_sem, piece_sem, share_sem, sent_pair, sent_fil, sent_near,
-     sent_fil_dp, sent_part, sent_out, sent_piece, sent_share) = refs[17:]
-    peers, _, count = pair_ref.shape[:3]
+    (fil_tokens, sig_tokens, cot_tokens, hold, pair_ready, fil_ready, pair_in, fil_in, rows, fil_rows, spec,
+     back_rows, pair_done, part, parts, summed) = refs[7:23]
+    (token_sem, table_sem, pair_sem, fil_sem, out_sem, part_sem, piece_sem, share_sem, sent_pair, sent_fil, sent_near,
+     sent_fil_dp, sent_part, sent_out, sent_piece, sent_share) = refs[23:]
+    peers = lax.axis_size("seq")
     replicas = lax.axis_size("dp")
     place = lax.axis_index("seq")
     replica = lax.axis_index("dp")
@@ -249,70 +248,72 @@
     def settle(like, sem):
         pltpu.make_async_copy(like, like, sem).wait()
 
+    inputs = [
+        pltpu.make_async_copy(source, target, token_sem.at[index])
+        for index, (source, target) in enumerate(zip(token_refs, (fil_tokens, sig_tokens, cot_tokens)))
+    ]
+    for load in inputs:
+        load.start()
     loads = [
         pltpu.make_async_copy(source, target, table_sem.at[index])
         for index, (source, target) in enumerate(zip(table_refs, tables))
     ]
+    barrier = pltpu.get_barrier_semaphore()
+
+    def greet(**where):
+        pl.semaphore_signal(barrier, 1, device_id=where, device_id_type=pl.DeviceIdType.MESH)
+
+    def greet_replica(step, carry):
+        greet(dp=lax.rem(replica + step, replicas))
+        return carry
+
+    each_partner(place, lambda to: greet(seq=to))
+    lax.fori_loop(1, replicas, greet_replica, 0)
+
+    unit = unit_ref[...]
+    columns = fil_tokens.shape[1] // LANES
+    inputs[0].wait()
+    for column in range(columns):
+        fil_ready[lane(column)] = flip(unit, fil_tokens, column, hold).astype(jnp.bfloat16)
+    inputs[1].wait()
+    inputs[2].wait()
+    keep = mask_ref[0, 0].astype(jnp.float32)
+    for column in range(columns):
+        sig = flip(unit, sig_tokens, column, hold) * keep
+        cot = flip(unit, cot_tokens, column, hold)
+        pair_ready[lane(column)] = jnp.concatenate([sig, cot], axis=1).astype(jnp.bfloat16)
+
+    def channels(to, half):
+        return pl.ds((to * HALVES + half) * count, count)
+
+    pl.semaphore_wait(barrier, peers - 1 + replicas - 1)
     for load in loads:
         load.start()
 
-    barrier = pltpu.get_barrier_semaphore()
-
-    def greet(step, carry):
-        pl.semaphore_signal(
-            barrier, 1, device_id={"seq": partner(place, step)}, device_id_type=pl.DeviceIdType.MESH
+    def filter_copy(to, sent):
+        return remote(
+            fil_ready.at[channels(to, own_half)], fil_in.at[own_half, place], sent, fil_sem.at[own_half], seq=to
         )
-        return carry
-
-    def greet_replica(step, carry):
-        pl.semaphore_signal(
-            barrier, 1, device_id={"dp": lax.rem(replica + step, replicas)}, device_id_type=pl.DeviceIdType.MESH
-        )
-        return carry
-
-    lax.fori_loop(1, peers, greet, 0)
-    lax.fori_loop(1, replicas, greet_replica, 0)
-    pl.semaphore_wait(barrier, peers - 1 + replicas - 1)
-
-    def filter_copy(to_chip):
-        to = to_chip * CORES + own_core
-        return remote(
-            solo_ref.at[to, own_half], fil_in.at[own_half, place], sent_fil, fil_sem.at[own_half], seq=to
-        )
-
-    def near_copy():
-        to = chip * CORES + own_core
-        return remote(
-            solo_ref.at[to, own_half], fil_in.at[own_half, place], sent_near, fil_sem.at[own_half], seq=to
-        )
-
-    def send_filter(step, carry):
-        filter_copy(partner_chip(place, step)).start()
-        return carry
-
-    lax.fori_loop(1, peers // CORES, send_filter, 0)
+
+    each_chip(place, lambda to: filter_copy(to * CORES + own_core, sent_fil).start())
 
     @pl.when(sharer)
     def _():
         pltpu.make_async_copy(
-            solo_ref.at[place, own_half], fil_in.at[own_half, place], fil_sem.at[own_half]
+            fil_ready.at[channels(place, own_half)], fil_in.at[own_half, place], fil_sem.at[own_half]
         ).start()
 
     @pl.when(jnp.logical_not(sharer))
     def _():
-        near_copy().start()
+        filter_copy(chip * CORES + own_core, sent_near).start()
 
     def send_pairs(half):
-        pltpu.make_async_copy(pair_ref.at[place, half], pair_in.at[half, place], pair_sem.at[half]).start()
-
-        def send(step, carry):
-            to = partner(place, step)
-            remote(
-                pair_ref.at[to, half], pair_in.at[half, place], sent_pair, pair_sem.at[half], seq=to
-            ).start()
-            return carry
-
-        lax.fori_loop(1, peers, send, 0)
+        pltpu.make_async_copy(
+            pair_ready.at[channels(place, half)], pair_in.at[half, place], pair_sem.at[half]
+        ).start()
+        each_partner(place, lambda to: remote(
+            pair_ready.at[channels(to, half)], pair_in.at[half, place], sent_pair, pair_sem.at[half], seq=to
+        ).start())
 
     send_pairs(0)
 
@@ -368,12 +369,9 @@
     def send_done(half):
         pltpu.make_async_copy(pair_done.at[half, place], pair_out.at[place, half], out_sem).start()
 
-        def send(step, carry):
-            to = partner(place, step)
-            remote(pair_done.at[half, to], pair_out.at[place, half], sent_out, out_sem, seq=to).start()
-            return carry
-
-        lax.fori_loop(1, peers, send, 0)
+        each_partner(place, lambda to: remote(
+            pair_done.at[half, to], pair_out.at[place, half], sent_out, out_sem, seq=to
+        ).start())
 
     def collect(half):
         @pl.when(replica == core * HALVES + half)
@@ -391,12 +389,9 @@
             lax.fori_loop(0, peers // ROWS, add, 0)
             pltpu.make_async_copy(summed.at[place], fil_out.at[chip, replica], piece_sem).start()
 
-            def send(step, carry):
-                to = partner(place, step)
-                remote(summed.at[to], fil_out.at[chip, replica], sent_piece, piece_sem, seq=to).start()
-                return carry
-
-            lax.fori_loop(1, peers, send, 0)
+            each_partner(place, lambda to: remote(
+                summed.at[to], fil_out.at[chip, replica], sent_piece, piece_sem, seq=to
+            ).start())
 
     settle(pair_in.at[0], pair_sem.at[0])
     transform(0)
@@ -422,8 +417,8 @@
     shares = fil_out.at[pl.ds(0, (replicas - 1) * peers // CORES // replicas)]
     settle(shares, share_sem)
     settle(pair_out, out_sem)
-    settle(pair_ref.at[pl.ds(0, peers - 1)], sent_pair)
-    settle(solo_ref.at[pl.ds(0, peers // CORES - 1), 0], sent_fil)
+    settle(pair_in.at[:, pl.ds(0, peers - 1)], sent_pair)
+    settle(fil_in.at[0, pl.ds(0, peers // CORES - 1)], sent_fil)
 
     @pl.when(sharer)
     def _():
@@ -443,59 +438,56 @@
     settle(shares, sent_share)
 
 
-def exchange(pair, solo, tables, factor):
-    peers, halves, count = pair.shape[:3]
+def exchange(block_mask, unit, filter_raw, signal, cotangent, tables, factor):
+    tokens, channels = filter_raw.shape
+    peers, replicas = lax.axis_size("seq"), lax.axis_size("dp")
+    count = channels // peers // HALVES
     height = tables[1].shape[2]
-    replicas = lax.axis_size("dp")
     whole = pl.BlockSpec(memory_space=pltpu.VMEM)
     anywhere = pl.BlockSpec(memory_space=pl.ANY)
     low = jnp.bfloat16
     tile, half_tile = (count, 2 * ROWS, LANES), (count, ROWS, LANES)
     dma = pltpu.SemaphoreType.DMA
     return pl.pallas_call(
-        functools.partial(exchange_body, factor),
-        in_specs=[anywhere] * 7,
-        out_specs=[whole] * 2,
+        functools.partial(exchange_body, factor, count),
+        in_specs=[pl.BlockSpec(memory_space=pltpu.SMEM), whole] + [anywhere] * 8,
+        out_specs=[anywhere] * 2,
         out_shape=[
-            jax.ShapeDtypeStruct(pair.shape, low),
+            jax.ShapeDtypeStruct((peers, HALVES) + tile, low),
             jax.ShapeDtypeStruct((peers // CORES, CORES * HALVES) + half_tile, low),
         ],
         scratch_shapes=[pltpu.VMEM(table.shape, table.dtype) for table in tables]
+        + [pltpu.VMEM((tokens, channels), low)] * 3
         + [
-            pltpu.VMEM((halves, peers) + tile, low),
-            pltpu.VMEM((halves, peers) + half_tile, low),
+            pltpu.VMEM((LANES * ROWS, LANES), jnp.float32),
+            pltpu.VMEM((channels, 2 * ROWS, LANES), low),
+            pltpu.VMEM((channels, ROWS, LANES), low),
+            pltpu.VMEM((HALVES, peers) + tile, low),
+            pltpu.VMEM((HALVES, peers) + half_tile, low),
             pltpu.VMEM((peers * ROWS, 2 * count * LANES), low),
             pltpu.VMEM((peers * ROWS, count * LANES), low),
-            pltpu.VMEM((halves, count, SLICES, height, 2 * LANES), jnp.float32),
+            pltpu.VMEM((HALVES, count, SLICES, height, 2 * LANES), jnp.float32),
             pltpu.VMEM((SLICES, 2 * height, 3 * count * LANES), low),
-            pltpu.VMEM((halves, peers) + tile, low),
-            pltpu.VMEM((halves, peers) + half_tile, low),
+            pltpu.VMEM((HALVES, peers) + tile, low),
+            pltpu.VMEM((HALVES, peers) + half_tile, low),
             pltpu.VMEM((replicas - 1, peers) + half_tile, low),
             pltpu.VMEM((peers,) + half_tile, low),
         ]
-        + [dma((len(tables),)), dma((halves,)), dma((halves,)), dma, dma, dma, dma, dma, dma, dma, dma,
-           dma((halves,)), dma, dma, dma],
+        + [dma((3,)), dma((len(tables),)), dma((HALVES,)), dma((HALVES,)), dma, dma, dma, dma, dma, dma, dma, dma,
+           dma((HALVES,)), dma, dma, dma],
         compiler_params=pltpu.CompilerParams(collective_id=0, has_side_effects=True),
         name="exchange",
-    )(pair, solo, *tables)
+    )(block_mask, unit, filter_raw, signal, cotangent, *tables)
 
 
 def per_device(signal, filter_raw, cotangent, block_mask):
     tokens, channels = filter_raw.shape
     peers = lax.axis_size("seq")
-    own = channels // peers
     tables = make_tables(peers * tokens // LANES)
     total = peers * tokens
     factor = 1.0 / (2 * total * math.sqrt(total))
     unit = jnp.asarray(np.eye(LANES, dtype=np.float32), jnp.bfloat16)
-    pair, solo = to_channels(block_mask, unit, signal[0], cotangent[0], filter_raw)
-    count = own // HALVES
-    pair, solo = exchange(
-        pair.reshape(peers, HALVES, count, 2 * ROWS, LANES),
-        solo.reshape(peers, HALVES, count, ROWS, LANES),
-        tables,
-        factor,
-    )
+    pair, solo = exchange(block_mask, unit, filter_raw, signal[0], cotangent[0], tables, factor)
     conv, grad, weight = to_tokens(
         block_mask, unit, pair.reshape(channels, 2 * ROWS, LANES), solo.reshape(channels, ROWS, LANES)
     )

time: 106 us -> 100 us (0.943)
  Pallas kernels: 105 us -> 98.9 us
    pallas_call x2 -> x1, Pallas kernels: 99.6 us -> 94 us  [exchange(): pl.pallas_call(functools.partial(exchange_body, factor, count), in_specs=...]
where the time goes in v2:
time: 100 us
  Pallas kernels  98.9 us (99%)
  between operations  1.29 us (1%)
    pallas_call x1, Pallas kernels, exchange(): pl.pallas_call(functools.partial(exchange_body, factor, count), in_specs=...  94 us
    pallas_call x1, Pallas kernels, to_tokens(): pl.pallas_call(scatter_body, grid=(channels // LANES,), in_specs=[pl.Bloc...  4.9 us

profile of v2, /device:TPU:1, one launch (start us, length us, event | category | flops | bytes accessed | tf_op | source)
XLA Modules:
  0.0 100.2 jit_solution(2134533691300446313)
XLA Ops:
  1.3 94.0 %exchange.1 = (bf16[64,2,3,16,128]{4,3,2,1,0:T(8,128)(2,1)}, bf16[32,4,3,8,128]{4,3,2,1,0:T(8,128)(2,1)}) custom-call(s32[1,1]{1,0:T(1,128)S(6)} %copy.13.mask_ref, bf16[128,128]{1,0:T(8,128)(2,1)} %constant.17.clone.unit_ref, bf16[1024,384]{1,0:T(8,128)(2,1)} %refs_0_.1, bf16[1024,384]{1,0:T(8,128)(2,1)} %bitcast.8, bf16[1024,384]{1,0:T(8,128)(2,1)} %bitcast.9, ...), custom_call_target="tpu_custom_call" | custom-call | tf_op jit(solution)/shard_map/exchange/pallas_call | solution.py:451
  95.3 4.9 %to_tokens.1 = (bf16[1024,384]{1,0:T(8,128)(2,1)}, bf16[1024,384]{1,0:T(8,128)(2,1)}, bf16[1024,384]{1,0:T(8,128)(2,1)}) custom-call(s32[1,1]{1,0:T(1,128)S(6)} %copy.13.mask_ref, bf16[128,128]{1,0:T(8,128)(2,1)} %constant.17.clone.unit_ref, bf16[384,16,128]{2,1,0:T(8,128)(2,1)} %bitcast.6, bf16[384,8,128]{2,1,0:T(8,128)(2,1)} %bitcast.7), custom_call_target="tpu_custom_call" | custom-call | tf_op jit(solution)/shard_map/to_tokens/pallas_call | solution.py:78
